TPU v7x, 256 devices: a whole 4x4x8 slice. The times are simulated.
256 devices in a mesh: seq: 32 (over y, z), grp: 8 (over x, core).
Axes of the slice: x: 4, y: 4, z: 8, core: 2. Of those that a mesh axis runs over, the one named last changes fastest.
Arguments:
- hidden: bfloat16 [16384, 2048], P('seq', 'grp'), may hold values from -8 to 8
- qkv_weight: bfloat16 [3, 2048, 6144], P(None, 'seq', 'grp'), may hold values from -0.125 to 0.125
- out_weight: bfloat16 [3, 2048, 2048], P(None, 'grp', 'seq'), may hold values from -0.125 to 0.125
- projection: float32 [3, 16, 128, 128], P(None, 'grp'), may hold values from -6 to 6
- norm_gain: float32 [3, 2048], replicated, may hold values from 0.1 to 1.9
- out_gain: float32 [3, 2048], P(None, 'grp'), may hold values from 0.1 to 1.9
Outputs:
- layer_out: bfloat16 [16384, 2048], P('seq', 'grp')
All inputs are finite; a program needn't handle non-finite values.
Results may differ from a plain program's by a relative error of at most 0.034.
Values may be sent and summed in bfloat16 or wider, within the bound.
No kernel may reach another device: no remote copies, remote signals or barrier semaphores. Data moves between devices by JAX's collectives and lax.ppermute only.
A program may use at most 64 MiB of HBM per device.

v0:
```python
import math
import jax
import jax.numpy as jnp
from jax import lax
from jax.sharding import Mesh
from jax.sharding import PartitionSpec as P

SEQ = ("seq_0", "seq_1")
stabilizer = 2.0
highest = lax.Precision.HIGHEST


def sent_to_all(array, axis):
    peers = lax.axis_size(axis)
    return lax.all_to_all(
        jnp.broadcast_to(array[None], (peers, *array.shape)), axis, 0, 0, tiled=True
    )


def joined_along(tiles, dim):
    lengths = list(tiles.shape[1:])
    lengths[dim] *= tiles.shape[0]
    return jnp.moveaxis(tiles, 0, dim).reshape(lengths)


def gathered_copies(array, axis, dim):
    tiles = sent_to_all(array, axis)
    return joined_along(tiles, dim)


def neutral_like(array, identity):
    return jax.tree.map(
        lambda a, e: jnp.broadcast_to(jnp.asarray(e, a.dtype), a.shape), array, identity
    )


def entering(array, axes, combine, identity):
    before = start = neutral_like(array, identity)
    subtotal = array
    for axis in reversed(axes):
        peers, index = (lax.axis_size(axis), lax.axis_index(axis))
        pieces = jax.tree.map(
            lambda part, kind: lax.all_gather(part.astype(kind), axis),
            subtotal,
            (jnp.bfloat16, jnp.bfloat16),
        )
        inside, subtotal = (start, start)
        for k in range(peers):
            passed = k < index
            subtotal = combine(
                subtotal, jax.tree.map(lambda part, own: part[k].astype(own.dtype), pieces, array)
            )
            inside = jax.tree.map(lambda new, old: jnp.where(passed, new, old), subtotal, inside)
        before = combine(inside, before)
    return before


def in_blocks(array, dim, peers):
    lengths = array.shape
    tiles = array.reshape(*lengths[:dim], peers, lengths[dim] // peers, *lengths[dim + 1 :])
    return jnp.moveaxis(tiles, dim, 0)


def sum_at_owner(array, axis, dim):
    tiles = in_blocks(array, dim, lax.axis_size(axis))
    arrived = lax.all_to_all(tiles, axis, split_axis=0, concat_axis=0, tiled=True)
    return arrived.astype(jnp.float32).sum(axis=0)


def features(rows, projection_layer):
    head_size = rows.shape[-1]
    feature_count = projection_layer.shape[-1]
    scaled = rows.astype(jnp.float32) * head_size ** (-0.25)
    mixed = jnp.einsum("thd,hdm->thm", scaled, projection_layer, precision=highest)
    energy = 0.5 * jnp.sum(scaled * scaled, axis=-1, keepdims=True)
    return (jnp.exp(mixed - energy - stabilizer) / math.sqrt(feature_count)).astype(jnp.bfloat16)


def add_states(earlier, later):
    return (earlier[0] + later[0], earlier[1] + later[1])


def local(hidden, qkv_weight, out_weight, projection, norm_gain, out_gain):
    layer_count = qkv_weight.shape[0]
    local_heads = projection.shape[1]
    head_size = projection.shape[2]
    feature_count = projection.shape[3]
    token_rows = hidden.shape[0]
    stream = hidden
    causal_mask = jnp.arange(token_rows)[:, None] >= jnp.arange(token_rows)[None, :]
    for layer_index in range(layer_count):
        gathered = gathered_copies(stream, "grp", 1)
        wide = gathered.astype(jnp.float32)
        inverse_rms = lax.rsqrt(jnp.mean(wide * wide, axis=-1, keepdims=True) + 1e-05)
        normed = (wide * inverse_rms * norm_gain[layer_index][None, :]).astype(jnp.bfloat16)
        qkv_wide = jnp.dot(
            normed,
            lax.all_gather(qkv_weight[layer_index], SEQ, axis=0, tiled=True),
            preferred_element_type=jnp.float32,
        )
        qkv = qkv_wide.astype(jnp.bfloat16).reshape(token_rows, local_heads, 3, head_size)
        query_feat = features(qkv[:, :, 0], projection[layer_index])
        key_feat = features(qkv[:, :, 1], projection[layer_index])
        value_rows = qkv[:, :, 2]
        block_kv = jnp.einsum(
            "jhm,jhe->hme", key_feat, value_rows, preferred_element_type=jnp.float32
        )
        block_z = jnp.sum(key_feat.astype(jnp.float32), axis=0)
        zero_kv = jnp.zeros((local_heads, feature_count, head_size), jnp.float32)
        zero_z = jnp.zeros((local_heads, feature_count), jnp.float32)
        prefix_kv, prefix_z = entering((block_kv, block_z), SEQ, add_states, (zero_kv, zero_z))
        scores = jnp.einsum(
            "ihm,jhm->hij", query_feat, key_feat, preferred_element_type=jnp.float32
        )
        masked = jnp.where(causal_mask[None], scores, jnp.zeros_like(scores))
        score_weights = masked.astype(jnp.bfloat16)
        query_wide = query_feat.astype(jnp.float32)
        denominator = jnp.sum(masked, axis=-1) + jnp.einsum(
            "ihm,hm->hi", query_wide, prefix_z, precision=highest
        )
        numerator = jnp.einsum(
            "hij,jhe->hie", score_weights, value_rows, preferred_element_type=jnp.float32
        )
        numerator = numerator + jnp.einsum(
            "ihm,hme->hie",
            query_feat,
            prefix_kv.astype(jnp.bfloat16),
            preferred_element_type=jnp.float32,
        )
        attention = numerator / denominator[..., None]
        inverse_norm = lax.rsqrt(jnp.mean(attention * attention, axis=-1, keepdims=True) + 1e-06)
        head_gain = out_gain[layer_index].reshape(local_heads, head_size)[:, None, :]
        attended = (attention * inverse_norm * head_gain).astype(jnp.bfloat16)
        attended = jnp.transpose(attended, (1, 0, 2)).reshape(token_rows, local_heads * head_size)
        terms = jnp.dot(
            attended,
            gathered_copies(out_weight[layer_index], SEQ, 1),
            preferred_element_type=jnp.float32,
        )
        summed = sum_at_owner(terms.astype(jnp.bfloat16), "grp", 1)
        stream = (stream.astype(jnp.float32) + summed).astype(jnp.bfloat16)
    return stream


def solution(mesh):
    finer = Mesh(mesh.devices.reshape(4, 8, mesh.shape["grp"]), ("seq_0", "seq_1", "grp"))
    in_specs = (
        P(SEQ, "grp"),
        P(None, SEQ, "grp"),
        P(None, "grp", SEQ),
        P(None, "grp", None, None),
        P(),
        P(None, "grp"),
    )
    out_specs = P(SEQ, "grp")
    return jax.shard_map(local, mesh=finer, in_specs=in_specs, out_specs=out_specs, check_vma=False)
```

profile of v0, /device:TPU:1, one launch (start us, length us, event | category | flops | bytes accessed | tf_op | source)
XLA Modules:
  0.0 526.0 jit_solution(9621818431269840428)
XLA Ops:
  6.5 1.7 fusion.264
  8.3 1.1 copy.52
  9.4 1.5 broadcast_in_dim.37
  10.9 6.9 %all-to-all-start = ((bf16[8,512,256]{1,2,0:T(8,128)(2,1)}), bf16[8,512,256]{1,2,0:T(8,128)(2,1)S(1)}, u32[]{:S(2)}, u32[]{:S(2)}) async-start(bf16[8,512,256]{1,2,0:T(8,128)(2,1)} %broadcast_in_dim.37), calls=%async_computation | async-start | bytes 4194304 | tf_op jit(solution)/shard_map/all_to_all | solution.py:15
  17.8 0.7 all-gather.18.cloned.1.call-update
  18.7 25.4 %all-to-all-done = bf16[8,512,256]{1,2,0:T(8,128)(2,1)S(1)} async-done(((bf16[8,512,256]{1,2,0:T(8,128)(2,1)}), bf16[8,512,256]{1,2,0:T(8,128)(2,1)S(1)}, u32[]{:S(2)}, u32[]{:S(2)}) %all-to-all-start) | async-done | bytes 2097184 | tf_op jit(solution)/shard_map/all_to_all | solution.py:15
  44.1 1.2 broadcast_in_dim.39
  45.3 10.2 %all-to-all-start.1 = ((bf16[32,256,64]{1,2,0:T(8,128)(2,1)}), bf16[32,256,64]{1,2,0:T(8,128)(2,1)S(1)}, u32[]{:S(2)}, u32[]{:S(2)}) async-start(bf16[32,256,64]{1,2,0:T(8,128)(2,1)} %broadcast_in_dim.39), calls=%async_computation.1 | async-start | bytes 2097152 | tf_op jit(solution)/shard_map/all_to_all | solution.py:15
  56.1 1.9 fusion.5
  58.0 42.3 %all-gather.16.cloned.1.call-done = bf16[1,2048,768]{2,1,0:T(8,128)(2,1)} async-done(((bf16[1,64,768]{2,1,0:T(8,128)(2,1)}), bf16[1,2048,768]{2,1,0:T(8,128)(2,1)}) %all-gather.16.cloned.1.call-update) | async-done | bytes 3145744 | tf_op jit(solution)/shard_map/all_gather | solution.py:98
  100.3 4.4 fusion.12
  105.9 0.7 fusion.50
  106.5 0.7 fusion.267
  107.2 10.7 %all-gather.9 = bf16[8,2,128]{2,1,0:T(2,128)(2,1)S(1)} all-gather(bf16[1,2,128]{2,1,0:T(2,128)(2,1)S(1)} %bitcast.627), channel_id=4, replica_groups=mesh['seq_0'=4,'seq_1'=8,'grp'=8] {'seq_1'}, dimensions={0}, use_global_device_ids=true | all-gather | bytes 4608 | tf_op jit(solution)/shard_map/all_gather | solution.py:43
  118.0 8.1 %all_gather.75 = bf16[4,2,128]{2,1,0:T(2,128)(2,1)S(1)} all-gather(bf16[1,2,128]{2,1,0:T(2,128)(2,1)S(1)} %fusion.246), channel_id=1, replica_groups=mesh['seq_0'=4,'seq_1'=8,'grp'=8] {'seq_0'}, dimensions={0}, use_global_device_ids=true | all-gather | bytes 2560 | tf_op jit(solution)/shard_map/all_gather | solution.py:43
  126.7 20.7 %all-gather.1 = bf16[16,128,128]{2,1,0:T(8,128)(2,1)S(1)} all-gather(bf16[2,128,128]{2,1,0:T(8,128)(2,1)S(1)} %convolution_convert_fusion.5), channel_id=3, replica_groups=mesh['seq_0'=4,'seq_1'=8,'grp'=8] {'seq_1'}, dimensions={0}, use_global_device_ids=true | all-gather | bytes 589824 | tf_op jit(solution)/shard_map/all_gather | solution.py:43
  147.5 10.9 %all_gather.72 = bf16[4,2,128,128]{3,2,1,0:T(8,128)(2,1)S(1)} all-gather(bf16[1,2,128,128]{3,2,1,0:T(8,128)(2,1)S(1)} %fusion.125), channel_id=1, replica_groups=mesh['seq_0'=4,'seq_1'=8,'grp'=8] {'seq_0'}, dimensions={0}, use_global_device_ids=true | all-gather | bytes 327680 | tf_op jit(solution)/shard_map/all_gather | solution.py:43
  159.8 0.8 convolution_convert_fusion.2
  160.7 44.9 %all_to_all.45 = bf16[8,512,256]{2,1,0:T(8,128)(2,1)S(1)} all-to-all(bf16[8,512,256]{2,1,0:T(8,128)(2,1)S(1)} %bitcast.597), channel_id=1, replica_groups=mesh['seq_0'=4,'seq_1'=8,'grp'=8] {'grp'}, dimensions={0} | all-to-all | bytes 4194304 | tf_op jit(solution)/shard_map/all_to_all | solution.py:66
  206.8 1.5 broadcast_in_dim.40
  208.3 4.5 all-to-all-start.3
  212.9 0.7 all-gather.20.cloned.1.call-update
  213.6 25.6 %all-to-all-done.3 = bf16[8,512,256]{1,2,0:T(8,128)(2,1)S(1)} async-done(((bf16[8,512,256]{1,2,0:T(8,128)(2,1)}), bf16[8,512,256]{1,2,0:T(8,128)(2,1)S(1)}, u32[]{:S(2)}, u32[]{:S(2)}) %all-to-all-start.3) | async-done | bytes 2097184 | tf_op jit(solution)/shard_map/all_to_all | solution.py:15
  239.2 1.2 broadcast_in_dim.42
  240.4 5.0 all-to-all-start.4
  245.9 1.9 fusion.3
  247.8 4.4 fusion.15
  253.4 1.7 fusion.268
  255.0 23.2 %all-gather.10 = bf16[8,2,128]{2,1,0:T(2,128)(2,1)S(1)} all-gather(bf16[1,2,128]{2,1,0:T(2,128)(2,1)S(1)} %bitcast.628), channel_id=7, replica_groups=mesh['seq_0'=4,'seq_1'=8,'grp'=8] {'seq_1'}, dimensions={0}, use_global_device_ids=true | all-gather | bytes 4608 | tf_op jit(solution)/shard_map/all_gather | solution.py:43
  278.3 8.0 %all_gather.82 = bf16[4,2,128]{2,1,0:T(2,128)(2,1)S(1)} all-gather(bf16[1,2,128]{2,1,0:T(2,128)(2,1)S(1)} %fusion.247), channel_id=1, replica_groups=mesh['seq_0'=4,'seq_1'=8,'grp'=8] {'seq_0'}, dimensions={0}, use_global_device_ids=true | all-gather | bytes 2560 | tf_op jit(solution)/shard_map/all_gather | solution.py:43
  286.5 21.1 %all-gather.4 = bf16[16,128,128]{2,1,0:T(8,128)(2,1)S(1)} all-gather(bf16[2,128,128]{2,1,0:T(8,128)(2,1)S(1)} %convolution_convert_fusion.4), channel_id=6, replica_groups=mesh['seq_0'=4,'seq_1'=8,'grp'=8] {'seq_1'}, dimensions={0}, use_global_device_ids=true | all-gather | bytes 589824 | tf_op jit(solution)/shard_map/all_gather | solution.py:43
  307.7 9.4 %all_gather.79 = bf16[4,2,128,128]{3,2,1,0:T(8,128)(2,1)S(1)} all-gather(bf16[1,2,128,128]{3,2,1,0:T(8,128)(2,1)S(1)} %fusion.124), channel_id=1, replica_groups=mesh['seq_0'=4,'seq_1'=8,'grp'=8] {'seq_0'}, dimensions={0}, use_global_device_ids=true | all-gather | bytes 327680 | tf_op jit(solution)/shard_map/all_gather | solution.py:43
  317.0 1.6 fusion.48
  320.4 0.8 convolution_convert_fusion.1
  321.3 42.6 %all_to_all.46 = bf16[8,512,256]{2,1,0:T(8,128)(2,1)S(1)} all-to-all(bf16[8,512,256]{2,1,0:T(8,128)(2,1)S(1)} %bitcast.598), channel_id=1, replica_groups=mesh['seq_0'=4,'seq_1'=8,'grp'=8] {'grp'}, dimensions={0} | all-to-all | bytes 4194304 | tf_op jit(solution)/shard_map/all_to_all | solution.py:66
  364.7 30.0 %all_to_all.47 = bf16[8,512,256]{1,2,0:T(8,128)(2,1)S(1)} all-to-all(bf16[8,512,256]{1,2,0:T(8,128)(2,1)S(1)} %broadcast_in_dim.43), channel_id=1, replica_groups=mesh['seq_0'=4,'seq_1'=8,'grp'=8] {'grp'}, dimensions={0} | all-to-all | bytes 4194304 | tf_op jit(solution)/shard_map/all_to_all | solution.py:15
  394.6 1.1 broadcast_in_dim.45
  395.7 6.9 %all-to-all-start.7 = ((bf16[32,256,64]{1,2,0:T(8,128)(2,1)}), bf16[32,256,64]{1,2,0:T(8,128)(2,1)S(1)}, u32[]{:S(2)}, u32[]{:S(2)}) async-start(bf16[32,256,64]{1,2,0:T(8,128)(2,1)} %broadcast_in_dim.45), calls=%async_computation.7 | async-start | bytes 2097152 | tf_op jit(solution)/shard_map/all_to_all | solution.py:15
  403.1 1.9 fusion.1
  405.0 4.4 fusion.18
  410.6 0.7 fusion.269
  411.3 21.4 %all-gather.11 = bf16[8,2,128]{2,1,0:T(2,128)(2,1)S(1)} all-gather(bf16[1,2,128]{2,1,0:T(2,128)(2,1)S(1)} %bitcast.629), channel_id=10, replica_groups=mesh['seq_0'=4,'seq_1'=8,'grp'=8] {'seq_1'}, dimensions={0}, use_global_device_ids=true | all-gather | bytes 4608 | tf_op jit(solution)/shard_map/all_gather | solution.py:43
  432.7 7.6 %all_gather.89 = bf16[4,2,128]{2,1,0:T(2,128)(2,1)S(1)} all-gather(bf16[1,2,128]{2,1,0:T(2,128)(2,1)S(1)} %fusion.248), channel_id=1, replica_groups=mesh['seq_0'=4,'seq_1'=8,'grp'=8] {'seq_0'}, dimensions={0}, use_global_device_ids=true | all-gather | bytes 2560 | tf_op jit(solution)/shard_map/all_gather | solution.py:43
  440.6 19.7 %all-gather.7 = bf16[16,128,128]{2,1,0:T(8,128)(2,1)S(1)} all-gather(bf16[2,128,128]{2,1,0:T(8,128)(2,1)S(1)} %convolution_convert_fusion.3), channel_id=9, replica_groups=mesh['seq_0'=4,'seq_1'=8,'grp'=8] {'seq_1'}, dimensions={0}, use_global_device_ids=true | all-gather | bytes 589824 | tf_op jit(solution)/shard_map/all_gather | solution.py:43
  460.4 9.4 %all_gather.86 = bf16[4,2,128,128]{3,2,1,0:T(8,128)(2,1)S(1)} all-gather(bf16[1,2,128,128]{3,2,1,0:T(8,128)(2,1)S(1)} %fusion.123), channel_id=1, replica_groups=mesh['seq_0'=4,'seq_1'=8,'grp'=8] {'seq_0'}, dimensions={0}, use_global_device_ids=true | all-gather | bytes 327680 | tf_op jit(solution)/shard_map/all_gather | solution.py:43
  472.3 0.8 convolution_convert_fusion
  473.2 44.6 %all_to_all.48 = bf16[8,512,256]{2,1,0:T(8,128)(2,1)S(1)} all-to-all(bf16[8,512,256]{2,1,0:T(8,128)(2,1)S(1)} %bitcast.599), channel_id=1, replica_groups=mesh['seq_0'=4,'seq_1'=8,'grp'=8] {'grp'}, dimensions={0} | all-to-all | bytes 4194304 | tf_op jit(solution)/shard_map/all_to_all | solution.py:66
  518.7 0.8 add_convert_fusion
  (110 shorter events, 15.2 us)
Async XLA Ops:
  6.5 93.8 %all-gather.16.cloned.1.call-start = ((), (), s32[]{:S(2)}) async-start(), calls=%async_computation.9 | async-start | bytes 3244032 | tf_op jit(solution)/shard_map/all_gather | solution.py:98
  10.9 7.7 %copy-start.8 = (f32[3,256]{1,0:T(4,128)S(1)}, f32[3,256]{1,0:T(4,128)}, u32[]{:S(2)}) copy-start(f32[3,256]{1,0:T(4,128)} %param.11) | copy-start | bytes 9220
  10.9 7.8 %copy-start.6 = (bf16[3,256,64]{1,2,0:T(8,128)(2,1)S(1)}, bf16[3,256,64]{1,2,0:T(8,128)(2,1)}, u32[]{:S(2)}) copy-start(bf16[3,256,64]{1,2,0:T(8,128)(2,1)} %param.8) | copy-start | bytes 294916
  10.9 7.8 %copy-start.7 = (f32[3,2048]{1,0:T(4,128)S(1)}, f32[3,2048]{1,0:T(4,128)}, u32[]{:S(2)}) copy-start(f32[3,2048]{1,0:T(4,128)} %param.10) | copy-start | bytes 73732
  10.9 33.2 %all-to-all-start = ((bf16[8,512,256]{1,2,0:T(8,128)(2,1)}), bf16[8,512,256]{1,2,0:T(8,128)(2,1)S(1)}, u32[]{:S(2)}, u32[]{:S(2)}) async-start(bf16[8,512,256]{1,2,0:T(8,128)(2,1)} %broadcast_in_dim.37), calls=%async_computation | async-start | bytes 4194304 | tf_op jit(solution)/shard_map/all_to_all | solution.py:15
  17.8 230.0 %all-gather.18.cloned.1.call-start = ((), (), s32[]{:S(2)}) async-start(), calls=%async_computation.10 | async-start | bytes 3244032 | tf_op jit(solution)/shard_map/all_gather | solution.py:98
  18.6 140.6 %copy-start.3 = (pred[512,512]{0,1:T(8,128)(4,1)}, pred[512,512]{0,1:T(8,128)(4,1)S(1)}, u32[]{:S(2)}) copy-start(pred[512,512]{0,1:T(8,128)(4,1)S(1)} %iota_compare_fusion) | copy-start | bytes 786436
  45.3 114.5 %all-to-all-start.1 = ((bf16[32,256,64]{1,2,0:T(8,128)(2,1)}), bf16[32,256,64]{1,2,0:T(8,128)(2,1)S(1)}, u32[]{:S(2)}, u32[]{:S(2)}) async-start(bf16[32,256,64]{1,2,0:T(8,128)(2,1)} %broadcast_in_dim.39), calls=%async_computation.1 | async-start | bytes 2097152 | tf_op jit(solution)/shard_map/all_to_all | solution.py:15
  104.7 1.2 copy-start.9
  205.7 1.0 copy-start.2
  208.3 30.9 %all-to-all-start.3 = ((bf16[8,512,256]{1,2,0:T(8,128)(2,1)}), bf16[8,512,256]{1,2,0:T(8,128)(2,1)S(1)}, u32[]{:S(2)}, u32[]{:S(2)}) async-start(bf16[8,512,256]{1,2,0:T(8,128)(2,1)} %broadcast_in_dim.40), calls=%async_computation.3 | async-start | bytes 4194304 | tf_op jit(solution)/shard_map/all_to_all | solution.py:15
  212.9 192.1 %all-gather.20.cloned.1.call-start = ((), (), s32[]{:S(2)}) async-start(), calls=%async_computation.11 | async-start | bytes 3244032 | tf_op jit(solution)/shard_map/all_gather | solution.py:98
  240.4 80.0 %all-to-all-start.4 = ((bf16[32,256,64]{1,2,0:T(8,128)(2,1)}), bf16[32,256,64]{1,2,0:T(8,128)(2,1)S(1)}, u32[]{:S(2)}, u32[]{:S(2)}) async-start(bf16[32,256,64]{1,2,0:T(8,128)(2,1)} %broadcast_in_dim.42), calls=%async_computation.4 | async-start | bytes 2097152 | tf_op jit(solution)/shard_map/all_to_all | solution.py:15
  253.3 65.6 %copy-start.4 = (pred[512,512]{0,1:T(8,128)(4,1)S(1)}, pred[512,512]{0,1:T(8,128)(4,1)}, u32[]{:S(2)}) copy-start(pred[512,512]{0,1:T(8,128)(4,1)} %copy-done.3) | copy-start | bytes 786436
  364.3 30.3 %copy-start = (bf16[512,256]{1,0:T(8,128)(2,1)}, bf16[512,256]{1,0:T(8,128)(2,1)S(1)}, u32[]{:S(2)}) copy-start(bf16[512,256]{1,0:T(8,128)(2,1)S(1)} %add_convert_fusion.1) | copy-start | bytes 786436
  395.7 76.6 %all-to-all-start.7 = ((bf16[32,256,64]{1,2,0:T(8,128)(2,1)}), bf16[32,256,64]{1,2,0:T(8,128)(2,1)S(1)}, u32[]{:S(2)}, u32[]{:S(2)}) async-start(bf16[32,256,64]{1,2,0:T(8,128)(2,1)} %broadcast_in_dim.45), calls=%async_computation.7 | async-start | bytes 2097152 | tf_op jit(solution)/shard_map/all_to_all | solution.py:15
  409.4 1.2 copy-start.10
  410.6 60.2 %copy-start.5 = (pred[512,512]{0,1:T(8,128)(4,1)S(1)}, pred[512,512]{0,1:T(8,128)(4,1)}, u32[]{:S(2)}) copy-start(pred[512,512]{0,1:T(8,128)(4,1)} %copy-done.3) | copy-start | bytes 786436
  517.8 1.0 copy-start.1
Sparse Core Ops, SparseCore 0:
  9.9 90.3 all-gather.15
  102.9 75.2 all-gather.17
  216.3 77.1 all-gather.19
where the time goes:
time: 527 us; the launch traced here: 526 us
  blocking collectives  332 us (63%)
  waiting for transfers between devices  94.8 us (18%)
  starting transfers between devices  33.5 us (6%)
  matrix products  27 us (5%)
  between operations  13.7 us (3%)
  local copies, waits for them, and re-layouts  13.5 us (3%)
  other arithmetic  11.1 us (2%)
    all_gather x12, blocking collectives, entering(): lax.all_gather(part.astype(kind), axis)  170 us
    all_to_all x3, blocking collectives, sum_at_owner(): lax.all_to_all(tiles, axis, split_axis=0, concat_axis=0, tiled=True)  132 us
    all_to_all x5, waiting for transfers between devices, sent_to_all(): lax.all_to_all(jnp.broadcast_to(array[None], (peers, *array.shape)), axis...  51 us
    all_gather x3, waiting for transfers between devices, local(): lax.all_gather(qkv_weight[layer_index], SEQ, axis=0, tiled=True)  42.3 us
    all_to_all x5, starting transfers between devices, sent_to_all(): lax.all_to_all(jnp.broadcast_to(array[None], (peers, *array.shape)), axis...  33.5 us
    all_to_all x1, blocking collectives, sent_to_all(): lax.all_to_all(jnp.broadcast_to(array[None], (peers, *array.shape)), axis...  30 us
    dot_general x3, matrix products, local(): jnp.dot(normed, lax.all_gather(qkv_weight[layer_index], SEQ, axis=0, tile...  13.1 us
  transfers between devices with their start and end apart: 8, of which 3 were waited for; matrix products, arithmetic and copies ran while one was open for 9% of the time, Pallas kernels for 0%

commit v1 on v0

--- a/solution.py
+++ b/solution.py
@@ -8,6 +8,13 @@
 SEQ = ("seq_0", "seq_1")
 stabilizer = 2.0
 highest = lax.Precision.HIGHEST
+
+
+def all_by_exchange(array, name, along):
+    count = lax.axis_size(name)
+    blocks = jnp.stack([array for _ in range(count)])
+    blocks = lax.all_to_all(blocks, name, split_axis=0, concat_axis=0)
+    return jnp.concatenate(blocks, axis=along)
 
 
 def sent_to_all(array, axis):
@@ -95,7 +102,7 @@
         normed = (wide * inverse_rms * norm_gain[layer_index][None, :]).astype(jnp.bfloat16)
         qkv_wide = jnp.dot(
             normed,
-            lax.all_gather(qkv_weight[layer_index], SEQ, axis=0, tiled=True),
+            all_by_exchange(qkv_weight[layer_index], SEQ, 0),
             preferred_element_type=jnp.float32,
         )
         qkv = qkv_wide.astype(jnp.bfloat16).reshape(token_rows, local_heads, 3, head_size)

time: 527 us -> 726 us (1.38)
  waiting for transfers between devices: 94.8 us -> 231 us
  blocking collectives: 332 us -> 374 us
  starting transfers between devices: 33.5 us -> 56.5 us
  between operations: 13.7 us -> 0.66 us
    all_to_all x0 -> x3, waiting for transfers between devices: none -> 205 us  [all_by_exchange(): blocks = lax.all_to_all(blocks, name, split_axis=0, concat_axis=0)]
    all_gather x3 -> x0, waiting for transfers between devices: 42.3 us -> none  [local(): lax.all_gather(qkv_weight[layer_index], SEQ, axis=0, tiled=True)]
    all_to_all x1 -> x2, blocking collectives: 30 us -> 59.9 us  [sent_to_all(): lax.all_to_all(jnp.broadcast_to(array[None], (peers, *array.shape)), axis...]
    all_to_all x5 -> x4, waiting for transfers between devices: 51 us -> 26.3 us  [sent_to_all(): lax.all_to_all(jnp.broadcast_to(array[None], (peers, *array.shape)), axis...]
    all_to_all x0 -> x3, starting transfers between devices: none -> 24.3 us  [all_by_exchange(): blocks = lax.all_to_all(blocks, name, split_axis=0, concat_axis=0)]
    all_gather x12, blocking collectives: 170 us -> 179 us  [entering(): lax.all_gather(part.astype(kind), axis)]
    all_to_all x5 -> x4, starting transfers between devices: 33.5 us -> 32.3 us  [sent_to_all(): lax.all_to_all(jnp.broadcast_to(array[None], (peers, *array.shape)), axis...]
  transfers between devices with their start and end apart: 8 -> 7, of which waited for: 3 -> 4; matrix products, arithmetic and copies ran while one was open for 9% -> 6% of each run, Pallas kernels for 0% -> 0%
where the time goes in v1:
time: 726 us; the launch traced here: 725 us
  blocking collectives  374 us (52%)
  waiting for transfers between devices  231 us (32%)
  starting transfers between devices  56.5 us (8%)
  matrix products  32.9 us (5%)
  local copies, waits for them, and re-layouts  18.4 us (3%)
  other arithmetic  11.8 us (2%)
    all_to_all x3, waiting for transfers between devices, all_by_exchange(): blocks = lax.all_to_all(blocks, name, split_axis=0, concat_axis=0)  205 us
    all_gather x12, blocking collectives, entering(): lax.all_gather(part.astype(kind), axis)  179 us
    all_to_all x3, blocking collectives, sum_at_owner(): lax.all_to_all(tiles, axis, split_axis=0, concat_axis=0, tiled=True)  135 us
    all_to_all x2, blocking collectives, sent_to_all(): lax.all_to_all(jnp.broadcast_to(array[None], (peers, *array.shape)), axis...  59.9 us
    all_to_all x4, starting transfers between devices, sent_to_all(): lax.all_to_all(jnp.broadcast_to(array[None], (peers, *array.shape)), axis...  32.3 us
    all_to_all x4, waiting for transfers between devices, sent_to_all(): lax.all_to_all(jnp.broadcast_to(array[None], (peers, *array.shape)), axis...  26.3 us
    all_to_all x3, starting transfers between devices, all_by_exchange(): blocks = lax.all_to_all(blocks, name, split_axis=0, concat_axis=0)  24.3 us
  transfers between devices with their start and end apart: 7, of which 4 were waited for; matrix products, arithmetic and copies ran while one was open for 6% of the time, Pallas kernels for 0%

profile of v1, /device:TPU:1, one launch (start us, length us, event | category | flops | bytes accessed | tf_op | source)
XLA Modules:
  0.0 725.1 jit_solution(15657649643887399041)
XLA Ops:
  1.1 1.5 broadcast_in_dim.37
  2.6 6.9 all-to-all-start
  9.5 26.3 %all-to-all-done = bf16[8,512,256]{1,2,0:T(8,128)(2,1)S(1)} async-done(((bf16[8,512,256]{1,2,0:T(8,128)(2,1)}), bf16[8,512,256]{1,2,0:T(8,128)(2,1)S(1)}, u32[]{:S(2)}, u32[]{:S(2)}) %all-to-all-start) | async-done | bytes 2097184 | tf_op jit(solution)/shard_map/all_to_all | solution.py:22
  35.9 2.1 stack.9
  37.9 10.5 %all-to-all-start.1 = ((bf16[32,64,768]{2,1,0:T(8,128)(2,1)}), bf16[32,64,768]{2,1,0:T(8,128)(2,1)}, u32[]{:S(2)}, u32[]{:S(2)}) async-start(bf16[32,64,768]{2,1,0:T(8,128)(2,1)} %stack.9), calls=%async_computation.1 | async-start | bytes 6291456 | tf_op jit(solution)/shard_map/all_to_all | solution.py:16
  49.9 1.9 fusion.2
  51.8 67.7 %all-to-all-done.1 = bf16[32,64,768]{2,1,0:T(8,128)(2,1)} async-done(((bf16[32,64,768]{2,1,0:T(8,128)(2,1)}), bf16[32,64,768]{2,1,0:T(8,128)(2,1)}, u32[]{:S(2)}, u32[]{:S(2)}) %all-to-all-start.1) | async-done | bytes 3145760 | tf_op jit(solution)/shard_map/all_to_all | solution.py:16
  119.4 1.1 broadcast_in_dim.39
  120.5 9.1 %all-to-all-start.2 = ((bf16[32,256,64]{1,2,0:T(8,128)(2,1)}), bf16[32,256,64]{1,2,0:T(8,128)(2,1)S(1)}, u32[]{:S(2)}, u32[]{:S(2)}) async-start(bf16[32,256,64]{1,2,0:T(8,128)(2,1)} %broadcast_in_dim.39), calls=%async_computation.2 | async-start | bytes 2097152 | tf_op jit(solution)/shard_map/all_to_all | solution.py:22
  129.6 4.6 convolution_convert_fusion.5
  134.3 1.4 copy.53
  136.1 1.6 fusion.253
  137.8 22.3 %all-gather.6 = bf16[8,2,128]{2,1,0:T(2,128)(2,1)S(1)} all-gather(bf16[1,2,128]{2,1,0:T(2,128)(2,1)S(1)} %bitcast.608), channel_id=3, replica_groups=mesh['seq_0'=4,'seq_1'=8,'grp'=8] {'seq_1'}, dimensions={0}, use_global_device_ids=true | all-gather | bytes 4608 | tf_op jit(solution)/shard_map/all_gather | solution.py:50
  160.0 7.5 %all_gather.65 = bf16[4,2,128]{2,1,0:T(2,128)(2,1)S(1)} all-gather(bf16[1,2,128]{2,1,0:T(2,128)(2,1)S(1)} %fusion.234), channel_id=1, replica_groups=mesh['seq_0'=4,'seq_1'=8,'grp'=8] {'seq_0'}, dimensions={0}, use_global_device_ids=true | all-gather | bytes 2560 | tf_op jit(solution)/shard_map/all_gather | solution.py:50
  168.2 19.6 %all-gather = bf16[16,128,128]{2,1,0:T(8,128)(2,1)S(1)} all-gather(bf16[2,128,128]{2,1,0:T(8,128)(2,1)S(1)} %convolution_convert_fusion.8), channel_id=2, replica_groups=mesh['seq_0'=4,'seq_1'=8,'grp'=8] {'seq_1'}, dimensions={0}, use_global_device_ids=true | all-gather | bytes 589824 | tf_op jit(solution)/shard_map/all_gather | solution.py:50
  187.9 9.4 %all_gather.62 = bf16[4,2,128,128]{3,2,1,0:T(8,128)(2,1)S(1)} all-gather(bf16[1,2,128,128]{3,2,1,0:T(8,128)(2,1)S(1)} %fusion.113), channel_id=1, replica_groups=mesh['seq_0'=4,'seq_1'=8,'grp'=8] {'seq_0'}, dimensions={0}, use_global_device_ids=true | all-gather | bytes 327680 | tf_op jit(solution)/shard_map/all_gather | solution.py:50
  197.3 1.6 fusion.38
  201.6 44.7 %all_to_all.60 = bf16[8,512,256]{2,1,0:T(8,128)(2,1)S(1)} all-to-all(bf16[8,512,256]{2,1,0:T(8,128)(2,1)S(1)} %bitcast.576), channel_id=1, replica_groups=mesh['seq_0'=4,'seq_1'=8,'grp'=8] {'grp'}, dimensions={0} | all-to-all | bytes 4194304 | tf_op jit(solution)/shard_map/all_to_all | solution.py:73
  247.7 30.0 %all_to_all.61 = bf16[8,512,256]{1,2,0:T(8,128)(2,1)S(1)} all-to-all(bf16[8,512,256]{1,2,0:T(8,128)(2,1)S(1)} %broadcast_in_dim.40), channel_id=1, replica_groups=mesh['seq_0'=4,'seq_1'=8,'grp'=8] {'grp'}, dimensions={0} | all-to-all | bytes 4194304 | tf_op jit(solution)/shard_map/all_to_all | solution.py:22
  277.6 2.1 stack.10
  279.7 6.7 all-to-all-start.5
  286.9 1.9 fusion.5
  288.8 68.5 %all-to-all-done.5 = bf16[32,64,768]{2,1,0:T(8,128)(2,1)} async-done(((bf16[32,64,768]{2,1,0:T(8,128)(2,1)}), bf16[32,64,768]{2,1,0:T(8,128)(2,1)}, u32[]{:S(2)}, u32[]{:S(2)}) %all-to-all-start.5) | async-done | bytes 3145760 | tf_op jit(solution)/shard_map/all_to_all | solution.py:16
  358.4 8.0 %all-to-all-start.6 = ((bf16[32,256,64]{1,2,0:T(8,128)(2,1)}), bf16[32,256,64]{1,2,0:T(8,128)(2,1)S(1)}, u32[]{:S(2)}, u32[]{:S(2)}) async-start(bf16[32,256,64]{1,2,0:T(8,128)(2,1)} %broadcast_in_dim.42), calls=%async_computation.6 | async-start | bytes 2097152 | tf_op jit(solution)/shard_map/all_to_all | solution.py:22
  366.4 4.4 convolution_convert_fusion.4
  371.5 1.6 fusion.254
  374.1 32.9 %all-gather.2 = bf16[16,128,128]{2,1,0:T(8,128)(2,1)S(1)} all-gather(bf16[2,128,128]{2,1,0:T(8,128)(2,1)S(1)} %convolution_convert_fusion.7), channel_id=4, replica_groups=mesh['seq_0'=4,'seq_1'=8,'grp'=8] {'seq_1'}, dimensions={0}, use_global_device_ids=true | all-gather | bytes 589824 | tf_op jit(solution)/shard_map/all_gather | solution.py:50
  407.5 10.2 %all-gather.7 = bf16[8,2,128]{2,1,0:T(2,128)(2,1)S(1)} all-gather(bf16[1,2,128]{2,1,0:T(2,128)(2,1)S(1)} %bitcast.606), channel_id=5, replica_groups=mesh['seq_0'=4,'seq_1'=8,'grp'=8] {'seq_1'}, dimensions={0}, use_global_device_ids=true | all-gather | bytes 4608 | tf_op jit(solution)/shard_map/all_gather | solution.py:50
  417.7 7.7 %all_gather.71 = bf16[4,2,128]{2,1,0:T(2,128)(2,1)S(1)} all-gather(bf16[1,2,128]{2,1,0:T(2,128)(2,1)S(1)} %fusion.235), channel_id=1, replica_groups=mesh['seq_0'=4,'seq_1'=8,'grp'=8] {'seq_0'}, dimensions={0}, use_global_device_ids=true | all-gather | bytes 2560 | tf_op jit(solution)/shard_map/all_gather | solution.py:50
  425.4 9.4 %all_gather.68 = bf16[4,2,128,128]{3,2,1,0:T(8,128)(2,1)S(1)} all-gather(bf16[1,2,128,128]{3,2,1,0:T(8,128)(2,1)S(1)} %fusion.112), channel_id=1, replica_groups=mesh['seq_0'=4,'seq_1'=8,'grp'=8] {'seq_0'}, dimensions={0}, use_global_device_ids=true | all-gather | bytes 327680 | tf_op jit(solution)/shard_map/all_gather | solution.py:50
  434.8 1.6 fusion.36
  436.7 1.6 select_reduce_fusion.1
  440.2 45.1 %all_to_all.62 = bf16[8,512,256]{2,1,0:T(8,128)(2,1)S(1)} all-to-all(bf16[8,512,256]{2,1,0:T(8,128)(2,1)S(1)} %bitcast.577), channel_id=1, replica_groups=mesh['seq_0'=4,'seq_1'=8,'grp'=8] {'grp'}, dimensions={0} | all-to-all | bytes 4194304 | tf_op jit(solution)/shard_map/all_to_all | solution.py:73
  486.0 30.0 %all_to_all.63 = bf16[8,512,256]{1,2,0:T(8,128)(2,1)S(1)} all-to-all(bf16[8,512,256]{1,2,0:T(8,128)(2,1)S(1)} %broadcast_in_dim.43), channel_id=1, replica_groups=mesh['seq_0'=4,'seq_1'=8,'grp'=8] {'grp'}, dimensions={0} | all-to-all | bytes 4194304 | tf_op jit(solution)/shard_map/all_to_all | solution.py:22
  515.9 2.1 stack.11
  518.0 7.1 all-to-all-start.9
  525.6 1.9 fusion.8
  527.5 68.7 %all-to-all-done.9 = bf16[32,64,768]{2,1,0:T(8,128)(2,1)} async-done(((bf16[32,64,768]{2,1,0:T(8,128)(2,1)}), bf16[32,64,768]{2,1,0:T(8,128)(2,1)}, u32[]{:S(2)}, u32[]{:S(2)}) %all-to-all-start.9) | async-done | bytes 3145760 | tf_op jit(solution)/shard_map/all_to_all | solution.py:16
  597.3 8.3 %all-to-all-start.10 = ((bf16[32,256,64]{1,2,0:T(8,128)(2,1)}), bf16[32,256,64]{1,2,0:T(8,128)(2,1)S(1)}, u32[]{:S(2)}, u32[]{:S(2)}) async-start(bf16[32,256,64]{1,2,0:T(8,128)(2,1)} %broadcast_in_dim.45), calls=%async_computation.10 | async-start | bytes 2097152 | tf_op jit(solution)/shard_map/all_to_all | solution.py:22
  605.6 4.4 convolution_convert_fusion.3
  610.7 1.6 fusion.255
  613.3 32.0 %all-gather.4 = bf16[16,128,128]{2,1,0:T(8,128)(2,1)S(1)} all-gather(bf16[2,128,128]{2,1,0:T(8,128)(2,1)S(1)} %convolution_convert_fusion.6), channel_id=6, replica_groups=mesh['seq_0'=4,'seq_1'=8,'grp'=8] {'seq_1'}, dimensions={0}, use_global_device_ids=true | all-gather | bytes 589824 | tf_op jit(solution)/shard_map/all_gather | solution.py:50
  645.8 11.0 %all-gather.8 = bf16[8,2,128]{2,1,0:T(2,128)(2,1)S(1)} all-gather(bf16[1,2,128]{2,1,0:T(2,128)(2,1)S(1)} %bitcast.607), channel_id=7, replica_groups=mesh['seq_0'=4,'seq_1'=8,'grp'=8] {'seq_1'}, dimensions={0}, use_global_device_ids=true | all-gather | bytes 4608 | tf_op jit(solution)/shard_map/all_gather | solution.py:50
  656.8 7.4 %all_gather.77 = bf16[4,2,128]{2,1,0:T(2,128)(2,1)S(1)} all-gather(bf16[1,2,128]{2,1,0:T(2,128)(2,1)S(1)} %fusion.236), channel_id=1, replica_groups=mesh['seq_0'=4,'seq_1'=8,'grp'=8] {'seq_0'}, dimensions={0}, use_global_device_ids=true | all-gather | bytes 2560 | tf_op jit(solution)/shard_map/all_gather | solution.py:50
  664.2 9.4 %all_gather.74 = bf16[4,2,128,128]{3,2,1,0:T(8,128)(2,1)S(1)} all-gather(bf16[1,2,128,128]{3,2,1,0:T(8,128)(2,1)S(1)} %fusion.111), channel_id=1, replica_groups=mesh['seq_0'=4,'seq_1'=8,'grp'=8] {'seq_0'}, dimensions={0}, use_global_device_ids=true | all-gather | bytes 327680 | tf_op jit(solution)/shard_map/all_gather | solution.py:50
  673.6 1.6 fusion.34
  675.4 1.5 select_reduce_fusion
  678.8 45.2 %all_to_all.64 = bf16[8,512,256]{2,1,0:T(8,128)(2,1)S(1)} all-to-all(bf16[8,512,256]{2,1,0:T(8,128)(2,1)S(1)} %bitcast.578), channel_id=1, replica_groups=mesh['seq_0'=4,'seq_1'=8,'grp'=8] {'grp'}, dimensions={0} | all-to-all | bytes 4194304 | tf_op jit(solution)/shard_map/all_to_all | solution.py:73
  (112 shorter events, 21.2 us)
Async XLA Ops:
  2.6 6.9 copy-start.2
  2.6 33.2 %all-to-all-start = ((bf16[8,512,256]{1,2,0:T(8,128)(2,1)}), bf16[8,512,256]{1,2,0:T(8,128)(2,1)S(1)}, u32[]{:S(2)}, u32[]{:S(2)}) async-start(bf16[8,512,256]{1,2,0:T(8,128)(2,1)} %broadcast_in_dim.37), calls=%async_computation | async-start | bytes 4194304 | tf_op jit(solution)/shard_map/all_to_all | solution.py:22
  37.9 10.5 %copy-start.9 = (f32[3,2048]{1,0:T(4,128)S(1)}, f32[3,2048]{1,0:T(4,128)}, u32[]{:S(2)}) copy-start(f32[3,2048]{1,0:T(4,128)} %param.10) | copy-start | bytes 73732
  37.9 11.4 %copy-start.10 = (f32[3,256]{1,0:T(4,128)S(1)}, f32[3,256]{1,0:T(4,128)}, u32[]{:S(2)}) copy-start(f32[3,256]{1,0:T(4,128)} %param.11) | copy-start | bytes 9220
  37.9 11.4 %copy-start.8 = (bf16[3,256,64]{1,2,0:T(8,128)(2,1)S(1)}, bf16[3,256,64]{1,2,0:T(8,128)(2,1)}, u32[]{:S(2)}) copy-start(bf16[3,256,64]{1,2,0:T(8,128)(2,1)} %param.8) | copy-start | bytes 294916
  37.9 81.5 %all-to-all-start.1 = ((bf16[32,64,768]{2,1,0:T(8,128)(2,1)}), bf16[32,64,768]{2,1,0:T(8,128)(2,1)}, u32[]{:S(2)}, u32[]{:S(2)}) async-start(bf16[32,64,768]{2,1,0:T(8,128)(2,1)} %stack.9), calls=%async_computation.1 | async-start | bytes 6291456 | tf_op jit(solution)/shard_map/all_to_all | solution.py:16
  51.8 77.9 %copy-start = (bf16[8,512,256]{1,2,0:T(8,128)(2,1)S(1)}, bf16[8,512,256]{1,2,0:T(8,128)(2,1)}, u32[]{:S(2)}) copy-start(bf16[8,512,256]{1,2,0:T(8,128)(2,1)} %fusion.2) | copy-start | bytes 6291460
  120.5 80.1 %all-to-all-start.2 = ((bf16[32,256,64]{1,2,0:T(8,128)(2,1)}), bf16[32,256,64]{1,2,0:T(8,128)(2,1)S(1)}, u32[]{:S(2)}, u32[]{:S(2)}) async-start(bf16[32,256,64]{1,2,0:T(8,128)(2,1)} %broadcast_in_dim.39), calls=%async_computation.2 | async-start | bytes 2097152 | tf_op jit(solution)/shard_map/all_to_all | solution.py:22
  137.7 61.4 %copy-start.3 = (pred[512,512]{0,1:T(8,128)(4,1)S(1)}, pred[512,512]{0,1:T(8,128)(4,1)}, u32[]{:S(2)}) copy-start(pred[512,512]{0,1:T(8,128)(4,1)} %iota_compare_fusion) | copy-start | bytes 786436
  246.3 1.0 copy-start.1
  279.7 77.6 %all-to-all-start.5 = ((bf16[32,64,768]{2,1,0:T(8,128)(2,1)}), bf16[32,64,768]{2,1,0:T(8,128)(2,1)}, u32[]{:S(2)}, u32[]{:S(2)}) async-start(bf16[32,64,768]{2,1,0:T(8,128)(2,1)} %stack.10), calls=%async_computation.5 | async-start | bytes 6291456 | tf_op jit(solution)/shard_map/all_to_all | solution.py:16
  358.4 80.9 %all-to-all-start.6 = ((bf16[32,256,64]{1,2,0:T(8,128)(2,1)}), bf16[32,256,64]{1,2,0:T(8,128)(2,1)S(1)}, u32[]{:S(2)}, u32[]{:S(2)}) async-start(bf16[32,256,64]{1,2,0:T(8,128)(2,1)} %broadcast_in_dim.42), calls=%async_computation.6 | async-start | bytes 2097152 | tf_op jit(solution)/shard_map/all_to_all | solution.py:22
  373.2 0.7 copy-start.6
  436.7 2.0 copy-start.4
  518.0 78.2 %all-to-all-start.9 = ((bf16[32,64,768]{2,1,0:T(8,128)(2,1)}), bf16[32,64,768]{2,1,0:T(8,128)(2,1)}, u32[]{:S(2)}, u32[]{:S(2)}) async-start(bf16[32,64,768]{2,1,0:T(8,128)(2,1)} %stack.11), calls=%async_computation.9 | async-start | bytes 6291456 | tf_op jit(solution)/shard_map/all_to_all | solution.py:16
  597.3 80.6 %all-to-all-start.10 = ((bf16[32,256,64]{1,2,0:T(8,128)(2,1)}), bf16[32,256,64]{1,2,0:T(8,128)(2,1)S(1)}, u32[]{:S(2)}, u32[]{:S(2)}) async-start(bf16[32,256,64]{1,2,0:T(8,128)(2,1)} %broadcast_in_dim.45), calls=%async_computation.10 | async-start | bytes 2097152 | tf_op jit(solution)/shard_map/all_to_all | solution.py:22
  612.3 0.7 copy-start.7
  612.3 63.1 %copy-start.5 = (pred[512,512]{0,1:T(8,128)(4,1)S(1)}, pred[512,512]{0,1:T(8,128)(4,1)}, u32[]{:S(2)}) copy-start(pred[512,512]{0,1:T(8,128)(4,1)} %iota_compare_fusion) | copy-start | bytes 786436
